TPU v7x, 256 devices: a whole 4x4x8 slice. The times are simulated.
256 devices in a mesh: seq: 16 (over y, x), exp: 16 (over z, core).
Axes of the slice: x: 4, y: 4, z: 8, core: 2. Of those that a mesh axis runs over, the one named last changes fastest.
Arguments:
- x_in: bfloat16 [4096, 8192], P('seq', 'exp'), may hold values from -6 to 6
- z_gate: bfloat16 [4096, 8192], P('seq', 'exp'), may hold values from -6 to 6
- b_in: bfloat16 [4096, 128], P('seq'), may hold values from -0.52734375 to 0.52734375
- c_out: bfloat16 [4096, 128], P('seq'), may hold values from -0.1875 to 0.1875
- dt_step: float32 [4096, 128], P('seq', 'exp'), may hold values from 0.12 to 2052, as said below
- rate: float32 [128], P('exp'), may hold values from 0 to 0.06, as said below
- skip: float32 [128], P('exp'), may hold values from 0.5 to 1.5
- init_state: float32 [128, 64, 128], P('exp'), may hold values from -16.970562 to 16.970562
- residual: bfloat16 [4096, 8192], P(('seq', 'exp')), may hold values from -6 to 6
- norm_gain: float32 [8192], replicated, may hold values from 0.5 to 1.5
- expert_ids: int32 [4096, 2], P(('seq', 'exp')), may hold values from 0 to 15, all different within a row; in each aligned block of 16 rows (0 to 15, 16 to 31, ...) at most 3 rows name the same one
- gate_weights: float32 [4096, 2], P(('seq', 'exp')), may hold values from 0.2 to 1
- w_gate: bfloat16 [16, 8192, 2048], P('exp', None, 'seq'), may hold values from -0.0625 to 0.0625
- w_up: bfloat16 [16, 8192, 2048], P('exp', None, 'seq'), may hold values from -0.0625 to 0.0625
- w_down: bfloat16 [16, 2048, 8192], P('exp', 'seq'), may hold values from -0.125 to 0.125
Outputs:
- layer_out: bfloat16 [4096, 8192], P(('seq', 'exp'))
Inputs may be any that keep to these rules, and one draw needn't show every extreme that they name: `dt_step`: positive step sizes. `rate`: positive rates. `expert_ids`: each row names two different experts; among the rows of one device (aligned blocks of 16 rows) no expert is named by more than 3 rows, and in every draw some expert is named by exactly 3 rows of some block.
All inputs are finite; a program needn't handle non-finite values.
Results may differ from a plain program's by a relative error of at most 0.0095.
Values may be sent and summed in bfloat16 or wider, within the bound.
A program may use at most 128 MiB of HBM per device.

v0:
```python
import jax
import jax.numpy as jnp
from jax import lax
from jax.sharding import PartitionSpec as P

GROUP = 128
PRECISE = lax.Precision.HIGHEST


def exclusive_scan(log, state, axis):
    devices = lax.axis_size(axis)
    inc = (log, state)
    exc = (jnp.zeros_like(log), jnp.zeros_like(state))
    shift = 1
    while shift < devices:
        pairs = [(i, i + shift) for i in range(devices - shift)]
        got = (lax.ppermute(inc[0], axis, pairs), lax.ppermute(inc[1], axis, pairs))
        exc = chain_combine(got, exc)
        inc = chain_combine(got, inc)
        shift *= 2
    return exc


def chain_combine(earlier, later):
    return (earlier[0] + later[0], jnp.exp(later[0])[:, None, None] * earlier[1] + later[1])


def on_device(
    x_in,
    z_gate,
    b_in,
    c_out,
    dt_step,
    rate,
    skip,
    init_state,
    residual,
    norm_gain,
    expert_ids,
    gate_weights,
    w_gate,
    w_up,
    w_down,
):
    token_count, channels = x_in.shape
    heads_here = rate.shape[0]
    head_width = channels // heads_here
    state_width = b_in.shape[1]
    blocks = token_count // GROUP
    inputs = x_in.astype(jnp.float32).reshape(blocks, GROUP, heads_here, head_width)
    keys_in = b_in.astype(jnp.float32).reshape(blocks, GROUP, state_width)
    queries = c_out.astype(jnp.float32).reshape(blocks, GROUP, state_width)
    log_steps = (-rate[None, :] * dt_step).reshape(blocks, GROUP, heads_here)
    cumulative = jnp.cumsum(log_steps, axis=1)
    scores = jnp.einsum("ctn,csn->cts", queries, keys_in, precision=PRECISE)
    causal = jnp.arange(GROUP)[:, None] >= jnp.arange(GROUP)[None, :]
    spread = cumulative[:, :, None, :] - cumulative[:, None, :, :]
    weights = jnp.exp(jnp.where(causal[None, :, :, None], spread, -jnp.inf)) * scores[..., None]
    intra_out = jnp.einsum("ctsh,cshp->cthp", weights, inputs, precision=PRECISE)
    tail_decay = jnp.exp(cumulative[:, -1:, :] - cumulative)
    block_state = jnp.einsum("csh,cshp,csn->chpn", tail_decay, inputs, keys_in, precision=PRECISE)
    block_log = cumulative[:, -1, :]

    def advance(carried, element):
        total_log, total_state = carried
        step_log, step_state = element
        updated = (
            total_log + step_log,
            jnp.exp(step_log)[:, None, None] * total_state + step_state,
        )
        return (updated, (total_log, total_state))

    zero_state = jnp.zeros((heads_here, head_width, state_width), jnp.float32)
    zero_log = jnp.zeros((heads_here,), jnp.float32)
    (device_log, device_state), (enter_log, enter_state) = lax.scan(
        advance, (zero_log, zero_state), (block_log, block_state)
    )
    prior_log, prior_state = exclusive_scan(device_log, device_state, "seq")
    incoming = prior_state + jnp.exp(prior_log)[:, None, None] * init_state
    entering = enter_state + jnp.exp(enter_log)[:, :, None, None] * incoming[None]
    inter_out = jnp.exp(cumulative)[..., None] * jnp.einsum(
        "chpn,ctn->cthp", entering, queries, precision=PRECISE
    )
    mixed_out = (intra_out + inter_out + skip[None, None, :, None] * inputs).reshape(
        token_count, channels
    )
    mixer = (mixed_out * jax.nn.silu(z_gate.astype(jnp.float32))).astype(jnp.bfloat16)
    token_mix = lax.all_to_all(mixer, "exp", split_axis=0, concat_axis=1, tiled=True)
    stream = (residual.astype(jnp.float32) + token_mix.astype(jnp.float32)).astype(jnp.bfloat16)
    widened = stream.astype(jnp.float32)
    normed = (
        widened
        * lax.rsqrt(jnp.mean(widened * widened, axis=-1, keepdims=True) + 1e-06)
        * norm_gain[None, :]
    ).astype(jnp.bfloat16)
    rows_here = residual.shape[0]
    owners = lax.axis_size("exp")
    local_experts = w_gate.shape[0]
    experts = owners * local_experts
    capacity = max(2, 2 * rows_here // experts + 1)
    width = residual.shape[1]
    chosen = expert_ids.reshape(-1)
    onehot = (chosen[:, None] == jnp.arange(experts)[None, :]).astype(jnp.int32)
    slot_index = jnp.sum((jnp.cumsum(onehot, axis=0) - onehot) * onehot, axis=1)
    target = slot_index * experts + chosen
    placing = (target[None, :] == jnp.arange(experts * capacity)[:, None]).astype(jnp.bfloat16)
    pair_rows = jnp.repeat(normed, 2, axis=0)
    outgoing = jnp.dot(placing, pair_rows, preferred_element_type=jnp.float32).astype(jnp.bfloat16)
    outgoing = outgoing.reshape(capacity, experts, width)
    arrived = lax.all_to_all(outgoing, "exp", split_axis=1, concat_axis=1, tiled=True)
    pieces = []
    for first, last in ((0, 1), (1, capacity)):
        chunk = arrived[first:last].reshape((last - first) * experts, width)
        segment = lax.all_gather(chunk, "seq", axis=0, tiled=True)
        gate_proj = jnp.dot(segment, w_gate[0], preferred_element_type=jnp.float32)
        up_proj = jnp.dot(segment, w_up[0], preferred_element_type=jnp.float32)
        active = (jax.nn.silu(gate_proj) * up_proj).astype(jnp.bfloat16)
        partial_value = jnp.dot(active, w_down[0], preferred_element_type=jnp.float32)
        pieces.append(
            lax.psum_scatter(
                partial_value.astype(jnp.bfloat16), "seq", scatter_dimension=0, tiled=True
            )
        )
    summed = jnp.concatenate(pieces, axis=0).reshape(capacity, experts, width)
    returned = lax.all_to_all(summed, "exp", split_axis=1, concat_axis=1, tiled=True)
    results = returned.reshape(experts * capacity, width)
    picked = results[target].astype(jnp.float32).reshape(rows_here, 2, width)
    mixture = jnp.sum(picked * gate_weights[:, :, None], axis=1)
    return (widened + mixture).astype(jnp.bfloat16)


def solution(mesh):
    return jax.shard_map(
        on_device,
        mesh=mesh,
        in_specs=(
            P("seq", "exp"),
            P("seq", "exp"),
            P("seq", None),
            P("seq", None),
            P("seq", "exp"),
            P("exp"),
            P("exp"),
            P("exp", None, None),
            P(("seq", "exp"), None),
            P(),
            P(("seq", "exp"), None),
            P(("seq", "exp"), None),
            P("exp", None, "seq"),
            P("exp", None, "seq"),
            P("exp", "seq", None),
        ),
        out_specs=P(("seq", "exp"), None),
        check_vma=False,
    )
```

profile of v0, /device:TPU:1, one launch (start us, length us, event | category | flops | bytes accessed | tf_op | source)
XLA Modules:
  0.0 493.9 jit_solution(8506652656855577056)
XLA Ops:
  11.2 1.8 while.17
  13.0 4.0 collective-permute-start.3
  17.0 3.1 collective-permute-start
  20.1 1.9 collective-permute-done
  22.1 5.6 %collective-permute-start.4 = (f32[8,64,128]{2,1,0:T(8,128)S(1)}, f32[8,64,128]{2,1,0:T(8,128)S(1)}, u32[]{:S(2)}, u32[]{:S(2)}) collective-permute-start(f32[8,64,128]{2,1,0:T(8,128)S(1)} %multiply_add_fusion.3), channel_id=1, source_target_pairs={{0,32},{16,48},{32,64},{48,80},{64,96},{80,112},{96,128},{112,144}... | collective-permute-start | bytes 786440 | tf_op jit(solution)/shard_map/ppermute | solution.py:17
  27.7 3.9 collective-permute-done.4
  31.7 7.2 %collective-permute-start.5 = (f32[8,64,128]{2,1,0:T(8,128)S(1)}, f32[8,64,128]{2,1,0:T(8,128)S(1)}, u32[]{:S(2)}, u32[]{:S(2)}) collective-permute-start(f32[8,64,128]{2,1,0:T(8,128)S(1)} %multiply_add_fusion.2), channel_id=1, source_target_pairs={{0,64},{16,80},{32,96},{48,112},{64,128},{80,144},{96,160},{112,17... | collective-permute-start | bytes 786440 | tf_op jit(solution)/shard_map/ppermute | solution.py:17
  38.9 1.7 fusion.77
  40.6 1.6 collective-permute-start.1
  44.3 9.5 %collective-permute-start.6 = (f32[8,64,128]{2,1,0:T(8,128)}, f32[8,64,128]{2,1,0:T(8,128)}, u32[]{:S(2)}, u32[]{:S(2)}) collective-permute-start(f32[8,64,128]{2,1,0:T(8,128)} %multiply_add_fusion.1), channel_id=1, source_target_pairs={{0,128},{16,144},{32,160},{48,176},{64,192},{80,208},{96,224},{112... | collective-permute-start | bytes 786440 | tf_op jit(solution)/shard_map/ppermute | solution.py:17
  60.2 3.3 collective-permute-start.7
  66.1 1.5 fusion.18
  67.6 2.2 fusion.17
  71.3 14.3 %all-to-all-start = ((bf16[16,16,512]{2,1,0:T(8,128)(2,1)}), bf16[16,16,512]{2,1,0:T(8,128)(2,1)S(1)}, u32[]{:S(2)}, u32[]{:S(2)}) async-start(bf16[16,16,512]{2,1,0:T(8,128)(2,1)} %bitcast.10), calls=%async_computation | async-start | bytes 524288 | tf_op jit(solution)/shard_map/all_to_all | solution.py:88
  86.0 11.3 %all-to-all-done = bf16[16,16,512]{2,1,0:T(8,128)(2,1)S(1)} async-done(((bf16[16,16,512]{2,1,0:T(8,128)(2,1)}), bf16[16,16,512]{2,1,0:T(8,128)(2,1)S(1)}, u32[]{:S(2)}, u32[]{:S(2)}) %all-to-all-start) | async-done | bytes 262176 | tf_op jit(solution)/shard_map/all_to_all | solution.py:88
  99.4 31.2 %all_to_all.23 = bf16[3,16,8192]{2,0,1:T(4,128)(2,1)S(1)} all-to-all(bf16[3,16,8192]{2,0,1:T(4,128)(2,1)S(1)} %copy.99), channel_id=1, replica_groups=mesh['seq'=16,'exp'=16] {'exp'}, dimensions={1} | all-to-all | bytes 1572864 | tf_op jit(solution)/shard_map/all_to_all | solution.py:110
  134.1 49.5 %all-gather.6.cloned.1.call-done = bf16[1,256,8192]{2,1,0:T(8,128)(2,1)} async-done(((bf16[1,16,8192]{2,1,0:T(8,128)(2,1)}), bf16[1,256,8192]{2,1,0:T(8,128)(2,1)}) %all-gather.6.cloned.1.call-update) | async-done | bytes 4194320 | tf_op jit(solution)/shard_map/all_gather | solution.py:114
  183.6 4.1 fusion.6
  187.7 7.3 %convolution_convert_fusion.1 = bf16[256,8192]{1,0:T(8,128)(2,1)} fusion(bf16[1,128,8192]{2,1,0:T(8,128)(2,1)S(1)} %copy-done, bf16[1,8192,128]{2,1,0:T(8,128)(2,1)} %param.30, bf16[1,256,8192]{2,1,0:T(8,128)(2,1)} %all-gather.6.cloned.1.call-done, f32[256,128]{1,0:T(8,128)S(1)} %fusion.6), kind=kOutput, calls=%fused_computation.10 | convolution fusion | flops 1076035584 | bytes 12713984 | tf_op jit(solution)/shard_map/dot_general | solution.py:118
  195.1 66.5 %all-gather.4.cloned.1.call-done = bf16[512,8192]{1,0:T(8,128)(2,1)} async-done(((bf16[32,8192]{1,0:T(8,128)(2,1)}), bf16[512,8192]{1,0:T(8,128)(2,1)}) %all-gather.4.cloned.1.call-update) | async-done | bytes 8388624 | tf_op jit(solution)/shard_map/all_gather | solution.py:114
  261.6 6.4 %fusion.13 = f32[512,128]{1,0:T(8,128)S(1)} fusion(bf16[512,8192]{1,0:T(8,128)(2,1)} %all-gather.4.cloned.1.call-done, bf16[1,8192,128]{2,1,0:T(8,128)(2,1)} %param.29), kind=kOutput, calls=%fused_computation.21 | convolution fusion | flops 1073741824 | bytes 10747904 | tf_op jit(solution)/shard_map/dot_general | solution.py:115
  268.6 2.3 fusion.22
  270.9 5.6 %convolution_convert_fusion = bf16[512,8192]{1,0:T(8,128)(2,1)} fusion(bf16[512,128]{1,0:T(8,128)(2,1)S(1)} %fusion.22, bf16[1,128,8192]{2,1,0:T(8,128)(2,1)S(1)} %copy-done), kind=kOutput, calls=%fused_computation.9 | convolution fusion | flops 1077936128 | bytes 10616832 | tf_op jit(solution)/shard_map/dot_general | solution.py:118
  276.5 69.4 %reduce-scatter.3.cloned.1.call-done = bf16[16,8192]{1,0:T(8,128)(2,1)} async-done(((bf16[256,8192]{1,0:T(8,128)(2,1)}), bf16[16,8192]{1,0:T(8,128)(2,1)}) %reduce-scatter.3.cloned.1.call-update) | async-done | bytes 262160 | tf_op jit(solution)/shard_map/reduce_scatter | solution.py:120
  345.9 94.2 %reduce-scatter.5.cloned.1.call-done = bf16[32,8192]{1,0:T(8,128)(2,1)} async-done(((bf16[512,8192]{1,0:T(8,128)(2,1)}), bf16[32,8192]{1,0:T(8,128)(2,1)}) %reduce-scatter.5.cloned.1.call-update) | async-done | bytes 524304 | tf_op jit(solution)/shard_map/reduce_scatter | solution.py:120
  441.4 1.7 copy.102
  443.0 9.0 %all-to-all-start.2 = ((bf16[3,16,8192]{2,0,1:T(4,128)(2,1)}), bf16[3,16,8192]{2,0,1:T(4,128)(2,1)}, u32[]{:S(2)}, u32[]{:S(2)}) async-start(bf16[3,16,8192]{2,0,1:T(4,128)(2,1)} %copy.102), calls=%async_computation.4 | async-start | bytes 2097152 | tf_op jit(solution)/shard_map/all_to_all | solution.py:125
  452.2 27.8 %all-to-all-done.2 = bf16[3,16,8192]{2,0,1:T(4,128)(2,1)} async-done(((bf16[3,16,8192]{2,0,1:T(4,128)(2,1)}), bf16[3,16,8192]{2,0,1:T(4,128)(2,1)}, u32[]{:S(2)}, u32[]{:S(2)}) %all-to-all-start.2) | async-done | bytes 786464 | tf_op jit(solution)/shard_map/all_to_all | solution.py:125
  480.0 1.8 copy.103
  481.8 1.7 gather_fusion
  483.5 1.7 reshape.142
  485.2 1.4 multiply_reduce_fusion
  (98 shorter events, 27.5 us)
Async XLA Ops:
  6.5 181.2 %copy-start = (bf16[1,128,8192]{2,1,0:T(8,128)(2,1)S(1)}, bf16[1,128,8192]{2,1,0:T(8,128)(2,1)}, u32[]{:S(2)}) copy-start(bf16[1,128,8192]{2,1,0:T(8,128)(2,1)} %param.31) | copy-start | bytes 6291460
  6.5 4.3 copy-start.3
  13.0 9.0 %collective-permute-start.3 = (f32[8,64,128]{2,1,0:T(8,128)S(1)}, f32[8,64,128]{2,1,0:T(8,128)S(1)}, u32[]{:S(2)}, u32[]{:S(2)}) collective-permute-start(f32[8,64,128]{2,1,0:T(8,128)S(1)} %get-tuple-element.48), channel_id=1, source_target_pairs={{0,16},{16,32},{32,48},{48,64},{64,80},{80,96},{96,112},{112,128},... | collective-permute-start | bytes 786440 | tf_op jit(solution)/shard_map/ppermute | solution.py:17
  17.0 5.0 %collective-permute-start = (f32[8]{0:T(128)S(1)}, f32[8]{0:T(128)S(1)}, u32[]{:S(2)}, u32[]{:S(2)}) collective-permute-start(f32[8]{0:T(128)S(1)} %get-tuple-element.47), channel_id=1, source_target_pairs={{0,16},{16,32},{32,48},{48,64},{64,80},{80,96},{96,112},{112,128},... | collective-permute-start | bytes 104 | tf_op jit(solution)/shard_map/ppermute | solution.py:17
  22.0 9.7 %copy-start.6 = (f32[8]{0:T(128)}, f32[8]{0:T(128)S(1)}, u32[]{:S(2)}) copy-start(f32[8]{0:T(128)S(1)} %collective-permute-done) | copy-start | bytes 100
  22.1 9.6 %collective-permute-start.4 = (f32[8,64,128]{2,1,0:T(8,128)S(1)}, f32[8,64,128]{2,1,0:T(8,128)S(1)}, u32[]{:S(2)}, u32[]{:S(2)}) collective-permute-start(f32[8,64,128]{2,1,0:T(8,128)S(1)} %multiply_add_fusion.3), channel_id=1, source_target_pairs={{0,32},{16,48},{32,64},{48,80},{64,96},{80,112},{96,128},{112,144}... | collective-permute-start | bytes 786440 | tf_op jit(solution)/shard_map/ppermute | solution.py:17
  31.7 11.8 %collective-permute-start.5 = (f32[8,64,128]{2,1,0:T(8,128)S(1)}, f32[8,64,128]{2,1,0:T(8,128)S(1)}, u32[]{:S(2)}, u32[]{:S(2)}) collective-permute-start(f32[8,64,128]{2,1,0:T(8,128)S(1)} %multiply_add_fusion.2), channel_id=1, source_target_pairs={{0,64},{16,80},{32,96},{48,112},{64,128},{80,144},{96,160},{112,17... | collective-permute-start | bytes 786440 | tf_op jit(solution)/shard_map/ppermute | solution.py:17
  40.6 2.3 collective-permute-start.1
  43.0 0.6 copy-start.7
  44.3 20.5 %collective-permute-start.6 = (f32[8,64,128]{2,1,0:T(8,128)}, f32[8,64,128]{2,1,0:T(8,128)}, u32[]{:S(2)}, u32[]{:S(2)}) collective-permute-start(f32[8,64,128]{2,1,0:T(8,128)} %multiply_add_fusion.1), channel_id=1, source_target_pairs={{0,128},{16,144},{32,160},{48,176},{64,192},{80,208},{96,224},{112... | collective-permute-start | bytes 786440 | tf_op jit(solution)/shard_map/ppermute | solution.py:17
  54.6 13.0 %copy-start.5 = (pred[128,128]{1,0:T(8,128)(4,1)S(1)}, pred[128,128]{1,0:T(8,128)(4,1)}, u32[]{:S(2)}) copy-start(pred[128,128]{1,0:T(8,128)(4,1)} %iota_compare_fusion) | copy-start | bytes 49156
  57.5 2.1 collective-permute-start.2
  60.2 4.0 collective-permute-start.7
  70.2 27.2 %copy-start.2 = (bf16[16,8192]{1,0:T(8,128)(2,1)S(1)}, bf16[16,8192]{1,0:T(8,128)(2,1)}, u32[]{:S(2)}) copy-start(bf16[16,8192]{1,0:T(8,128)(2,1)} %param.25) | copy-start | bytes 786436
  70.4 27.2 %copy-start.4 = (f32[8192]{0:T(1024)S(1)}, f32[8192]{0:T(1024)}, u32[]{:S(2)}) copy-start(f32[8192]{0:T(1024)} %param.26) | copy-start | bytes 98308
  71.3 26.0 %all-to-all-start = ((bf16[16,16,512]{2,1,0:T(8,128)(2,1)}), bf16[16,16,512]{2,1,0:T(8,128)(2,1)S(1)}, u32[]{:S(2)}, u32[]{:S(2)}) async-start(bf16[16,16,512]{2,1,0:T(8,128)(2,1)} %bitcast.10), calls=%async_computation | async-start | bytes 524288 | tf_op jit(solution)/shard_map/all_to_all | solution.py:88
  85.6 98.0 %all-gather.6.cloned.1.call-start = ((), (), s32[]{:S(2)}) async-start(), calls=%async_computation.8 | async-start | bytes 4456448 | tf_op jit(solution)/shard_map/all_gather | solution.py:114
  132.1 129.5 %all-gather.4.cloned.1.call-start = ((), (), s32[]{:S(2)}) async-start(), calls=%async_computation.6 | async-start | bytes 8912896 | tf_op jit(solution)/shard_map/all_gather | solution.py:114
  133.9 212.1 %reduce-scatter.3.cloned.1.call-start = ((), (), s32[]{:S(2)}) async-start(), calls=%async_computation.5 | async-start | bytes 4456448 | tf_op jit(solution)/shard_map/reduce_scatter | solution.py:120
  195.0 245.2 %reduce-scatter.5.cloned.1.call-start = ((), (), s32[]{:S(2)}) async-start(), calls=%async_computation.7 | async-start | bytes 8912896 | tf_op jit(solution)/shard_map/reduce_scatter | solution.py:120
  261.6 6.5 %copy-start.1 = (bf16[1,8192,128]{2,1,0:T(8,128)(2,1)S(1)}, bf16[1,8192,128]{2,1,0:T(8,128)(2,1)}, u32[]{:S(2)}) copy-start(bf16[1,8192,128]{2,1,0:T(8,128)(2,1)} %param.30) | copy-start | bytes 6291460
  261.6 7.0 %copy-start.9 = (bf16[512,8192]{1,0:T(8,128)(2,1)S(1)}, bf16[512,8192]{1,0:T(8,128)(2,1)}, u32[]{:S(2)}) copy-start(bf16[512,8192]{1,0:T(8,128)(2,1)} %all-gather.4.cloned.1.call-done) | copy-start | bytes 25165828
  441.4 10.7 %copy-start.8 = (f32[16,2]{0,1:T(2,128)S(1)}, f32[16,2]{0,1:T(2,128)}, u32[]{:S(2)}) copy-start(f32[16,2]{0,1:T(2,128)} %param.28) | copy-start | bytes 388
  443.0 37.0 %all-to-all-start.2 = ((bf16[3,16,8192]{2,0,1:T(4,128)(2,1)}), bf16[3,16,8192]{2,0,1:T(4,128)(2,1)}, u32[]{:S(2)}, u32[]{:S(2)}) async-start(bf16[3,16,8192]{2,0,1:T(4,128)(2,1)} %copy.102), calls=%async_computation.4 | async-start | bytes 2097152 | tf_op jit(solution)/shard_map/all_to_all | solution.py:125
Sparse Core Ops, SparseCore 0:
  132.2 51.3 all-gather.5
  186.0 75.4 all-gather.3
  265.2 80.6 reduce-scatter.2
  350.0 90.1 reduce-scatter.4
where the time goes:
time: 495 us; the launch traced here: 494 us
  waiting for transfers between devices  327 us (66%)
  starting transfers between devices  59.2 us (12%)
  matrix products  31.9 us (6%)
  blocking collectives  31.2 us (6%)
  local copies, waits for them, and re-layouts  18.1 us (4%)
  between operations  13.5 us (3%)
  other arithmetic  13 us (3%)
    reduce_scatter x2, waiting for transfers between devices, on_device(): lax.psum_scatter(partial_value.astype(jnp.bfloat16), 'seq', scatter_dimen...  164 us
    all_gather x2, waiting for transfers between devices, on_device(): segment = lax.all_gather(chunk, 'seq', axis=0, tiled=True)  116 us
    ppermute x8, starting transfers between devices, exclusive_scan(): got = (lax.ppermute(inc[0], axis, pairs), lax.ppermute(inc[1], axis, pairs))  35.6 us
    all_to_all x1, blocking collectives, on_device(): lax.all_to_all(outgoing, 'exp', split_axis=1, concat_axis=1, tiled=True)  31.2 us
    all_to_all x1, waiting for transfers between devices, on_device(): lax.all_to_all(summed, 'exp', split_axis=1, concat_axis=1, tiled=True)  27.8 us
    all_to_all x1, starting transfers between devices, on_device(): lax.all_to_all(mixer, 'exp', split_axis=0, concat_axis=1, tiled=True)  14.3 us
    dot_general x2, matrix products, on_device(): jnp.dot(active, w_down[0], preferred_element_type=jnp.float32)  12.8 us
    all_to_all x1, waiting for transfers between devices, on_device(): lax.all_to_all(mixer, 'exp', split_axis=0, concat_axis=1, tiled=True)  11.3 us
  transfers between devices with their start and end apart: 14, of which 11 were waited for; matrix products, arithmetic and copies ran while one was open for 7% of the time, Pallas kernels for 0%

commit v1 on v0

--- a/solution.py
+++ b/solution.py
@@ -111,7 +111,9 @@
     pieces = []
     for first, last in ((0, 1), (1, capacity)):
         chunk = arrived[first:last].reshape((last - first) * experts, width)
-        segment = lax.all_gather(chunk, "seq", axis=0, tiled=True)
+        segment = jnp.concatenate(
+            lax.all_to_all(jnp.stack([chunk] * lax.axis_size("seq")), "seq", 0, 0), axis=0
+        )
         gate_proj = jnp.dot(segment, w_gate[0], preferred_element_type=jnp.float32)
         up_proj = jnp.dot(segment, w_up[0], preferred_element_type=jnp.float32)
         active = (jax.nn.silu(gate_proj) * up_proj).astype(jnp.bfloat16)

time: 495 us -> 531 us (1.073)
  waiting for transfers between devices: 327 us -> 345 us
  starting transfers between devices: 59.2 us -> 68.4 us
    all_to_all x0 -> x2, waiting for transfers between devices: none -> 187 us  [on_device(): lax.all_to_all(jnp.stack([chunk] * lax.axis_size('seq')), 'seq', 0, 0)]
    all_gather x2 -> x0, waiting for transfers between devices: 116 us -> none  [on_device(): segment = lax.all_gather(chunk, 'seq', axis=0, tiled=True)]
    reduce_scatter x2, waiting for transfers between devices: 164 us -> 110 us  [on_device(): lax.psum_scatter(partial_value.astype(jnp.bfloat16), 'seq', scatter_dimen...]
    all_to_all x0 -> x2, starting transfers between devices: none -> 9.64 us  [on_device(): lax.all_to_all(jnp.stack([chunk] * lax.axis_size('seq')), 'seq', 0, 0)]
    another operation x0 -> x2, local copies, waits for them, and re-layouts: none -> 6.7 us  [on_device(): jnp.stack([chunk] * lax.axis_size('seq'))]
where the time goes in v1:
time: 531 us; the launch traced here: 530 us
  waiting for transfers between devices  345 us (65%)
  starting transfers between devices  68.4 us (13%)
  matrix products  35.5 us (7%)
  blocking collectives  31.2 us (6%)
  local copies, waits for them, and re-layouts  22.8 us (4%)
  between operations  13.8 us (3%)
  other arithmetic  13.1 us (2%)
    all_to_all x2, waiting for transfers between devices, on_device(): lax.all_to_all(jnp.stack([chunk] * lax.axis_size('seq')), 'seq', 0, 0)  187 us
    reduce_scatter x2, waiting for transfers between devices, on_device(): lax.psum_scatter(partial_value.astype(jnp.bfloat16), 'seq', scatter_dimen...  110 us
    ppermute x8, starting transfers between devices, exclusive_scan(): got = (lax.ppermute(inc[0], axis, pairs), lax.ppermute(inc[1], axis, pairs))  35.6 us
    all_to_all x1, blocking collectives, on_device(): lax.all_to_all(outgoing, 'exp', split_axis=1, concat_axis=1, tiled=True)  31.2 us
    all_to_all x1, waiting for transfers between devices, on_device(): lax.all_to_all(summed, 'exp', split_axis=1, concat_axis=1, tiled=True)  27.8 us
    all_to_all x1, starting transfers between devices, on_device(): lax.all_to_all(mixer, 'exp', split_axis=0, concat_axis=1, tiled=True)  14 us
    dot_general x2, matrix products, on_device(): jnp.dot(active, w_down[0], preferred_element_type=jnp.float32)  12.8 us
    all_to_all x1, waiting for transfers between devices, on_device(): lax.all_to_all(mixer, 'exp', split_axis=0, concat_axis=1, tiled=True)  11.4 us
  transfers between devices with their start and end apart: 14, of which 11 were waited for; matrix products, arithmetic and copies ran while one was open for 7% of the time, Pallas kernels for 0%

profile of v1, /device:TPU:1, one launch (start us, length us, event | category | flops | bytes accessed | tf_op | source)
XLA Modules:
  0.0 529.6 jit_solution(6539703627572766895)
XLA Ops:
  11.2 1.8 while.17
  13.0 4.0 collective-permute-start.3
  17.0 3.1 collective-permute-start
  20.1 1.9 collective-permute-done
  22.1 5.6 %collective-permute-start.4 = (f32[8,64,128]{2,1,0:T(8,128)S(1)}, f32[8,64,128]{2,1,0:T(8,128)S(1)}, u32[]{:S(2)}, u32[]{:S(2)}) collective-permute-start(f32[8,64,128]{2,1,0:T(8,128)S(1)} %multiply_add_fusion.3), channel_id=1, source_target_pairs={{0,32},{16,48},{32,64},{48,80},{64,96},{80,112},{96,128},{112,144}... | collective-permute-start | bytes 786440 | tf_op jit(solution)/shard_map/ppermute | solution.py:17
  27.7 3.9 collective-permute-done.4
  31.7 7.2 %collective-permute-start.5 = (f32[8,64,128]{2,1,0:T(8,128)S(1)}, f32[8,64,128]{2,1,0:T(8,128)S(1)}, u32[]{:S(2)}, u32[]{:S(2)}) collective-permute-start(f32[8,64,128]{2,1,0:T(8,128)S(1)} %multiply_add_fusion.2), channel_id=1, source_target_pairs={{0,64},{16,80},{32,96},{48,112},{64,128},{80,144},{96,160},{112,17... | collective-permute-start | bytes 786440 | tf_op jit(solution)/shard_map/ppermute | solution.py:17
  38.9 1.7 fusion.69
  44.4 9.5 %collective-permute-start.6 = (f32[8,64,128]{2,1,0:T(8,128)}, f32[8,64,128]{2,1,0:T(8,128)}, u32[]{:S(2)}, u32[]{:S(2)}) collective-permute-start(f32[8,64,128]{2,1,0:T(8,128)} %multiply_add_fusion.1), channel_id=1, source_target_pairs={{0,128},{16,144},{32,160},{48,176},{64,192},{80,208},{96,224},{112... | collective-permute-start | bytes 786440 | tf_op jit(solution)/shard_map/ppermute | solution.py:17
  60.4 3.3 collective-permute-start.7
  67.8 2.2 fusion.15
  71.4 14.0 %all-to-all-start = ((bf16[16,16,512]{2,1,0:T(8,128)(2,1)}), bf16[16,16,512]{2,1,0:T(8,128)(2,1)S(1)}, u32[]{:S(2)}, u32[]{:S(2)}) async-start(bf16[16,16,512]{2,1,0:T(8,128)(2,1)} %bitcast.10), calls=%async_computation | async-start | bytes 524288 | tf_op jit(solution)/shard_map/all_to_all | solution.py:88
  85.8 11.4 %all-to-all-done = bf16[16,16,512]{2,1,0:T(8,128)(2,1)S(1)} async-done(((bf16[16,16,512]{2,1,0:T(8,128)(2,1)}), bf16[16,16,512]{2,1,0:T(8,128)(2,1)S(1)}, u32[]{:S(2)}, u32[]{:S(2)}) %all-to-all-start) | async-done | bytes 262176 | tf_op jit(solution)/shard_map/all_to_all | solution.py:88
  99.3 31.2 %all_to_all.33 = bf16[3,16,8192]{2,0,1:T(4,128)(2,1)S(1)} all-to-all(bf16[3,16,8192]{2,0,1:T(4,128)(2,1)S(1)} %copy.99), channel_id=1, replica_groups=mesh['seq'=16,'exp'=16] {'exp'}, dimensions={1} | all-to-all | bytes 1572864 | tf_op jit(solution)/shard_map/all_to_all | solution.py:110
  131.2 2.4 stack.6
  133.7 4.9 all-to-all-start.2
  139.5 63.9 %all-to-all-done.2 = bf16[16,16,8192]{2,1,0:T(8,128)(2,1)} async-done(((bf16[16,16,8192]{2,1,0:T(8,128)(2,1)}), bf16[16,16,8192]{2,1,0:T(8,128)(2,1)}, u32[]{:S(2)}, u32[]{:S(2)}) %all-to-all-start.2) | async-done | bytes 4194336 | tf_op jit(solution)/shard_map/all_to_all | solution.py:115
  203.4 4.3 stack.7
  207.7 4.7 all-to-all-start.3
  212.6 4.1 fusion.12
  216.8 7.2 %convolution_convert_fusion.1 = bf16[256,8192]{1,0:T(8,128)(2,1)} fusion(bf16[1,128,8192]{2,1,0:T(8,128)(2,1)S(1)} %copy-done, bf16[256,8192]{1,0:T(8,128)(2,1)} %bitcast.14, bf16[1,8192,128]{2,1,0:T(8,128)(2,1)} %param.30, f32[256,128]{1,0:T(8,128)S(1)} %fusion.12), kind=kOutput, calls=%fused_computation.10 | convolution fusion | flops 1076035584 | bytes 12713984 | tf_op jit(solution)/shard_map/dot_general | solution.py:120
  224.1 123.6 %all-to-all-done.3 = bf16[16,32,8192]{2,1,0:T(8,128)(2,1)} async-done(((bf16[16,32,8192]{2,1,0:T(8,128)(2,1)}), bf16[16,32,8192]{2,1,0:T(8,128)(2,1)}, u32[]{:S(2)}, u32[]{:S(2)}) %all-to-all-start.3) | async-done | bytes 8388640 | tf_op jit(solution)/shard_map/all_to_all | solution.py:115
  347.7 6.6 %fusion.10 = f32[512,128]{1,0:T(8,128)S(1)} fusion(bf16[512,8192]{1,0:T(8,128)(2,1)} %bitcast.19, bf16[1,8192,128]{2,1,0:T(8,128)(2,1)} %param.29), kind=kOutput, calls=%fused_computation.18 | convolution fusion | flops 1073741824 | bytes 10747904 | tf_op jit(solution)/shard_map/dot_general | solution.py:117
  354.3 5.8 %fusion.20 = bf16[512,128]{1,0:T(8,128)(2,1)S(1)} fusion(bf16[512,8192]{1,0:T(8,128)(2,1)} %bitcast.19, bf16[1,8192,128]{2,1,0:T(8,128)(2,1)S(1)} %copy-done.1, f32[512,128]{1,0:T(8,128)S(1)} %fusion.10), kind=kOutput, calls=%fused_computation.28 | convolution fusion | flops 1074135040 | bytes 10878976 | tf_op jit(solution)/shard_map/dot_general | solution.py:118
  360.1 5.6 %convolution_convert_fusion = bf16[512,8192]{1,0:T(8,128)(2,1)} fusion(bf16[512,128]{1,0:T(8,128)(2,1)S(1)} %fusion.20, bf16[1,128,8192]{2,1,0:T(8,128)(2,1)S(1)} %copy-done), kind=kOutput, calls=%fused_computation.9 | convolution fusion | flops 1077936128 | bytes 10616832 | tf_op jit(solution)/shard_map/dot_general | solution.py:120
  365.7 15.6 %reduce-scatter.3.cloned.1.call-done = bf16[16,8192]{1,0:T(8,128)(2,1)} async-done(((bf16[256,8192]{1,0:T(8,128)(2,1)}), bf16[16,8192]{1,0:T(8,128)(2,1)}) %reduce-scatter.3.cloned.1.call-update) | async-done | bytes 262160 | tf_op jit(solution)/shard_map/reduce_scatter | solution.py:122
  381.3 94.3 %reduce-scatter.5.cloned.1.call-done = bf16[32,8192]{1,0:T(8,128)(2,1)} async-done(((bf16[512,8192]{1,0:T(8,128)(2,1)}), bf16[32,8192]{1,0:T(8,128)(2,1)}) %reduce-scatter.5.cloned.1.call-update) | async-done | bytes 524304 | tf_op jit(solution)/shard_map/reduce_scatter | solution.py:122
  476.8 1.7 copy.102
  478.5 8.9 %all-to-all-start.4 = ((bf16[3,16,8192]{2,0,1:T(4,128)(2,1)}), bf16[3,16,8192]{2,0,1:T(4,128)(2,1)}, u32[]{:S(2)}, u32[]{:S(2)}) async-start(bf16[3,16,8192]{2,0,1:T(4,128)(2,1)} %copy.102), calls=%async_computation.6 | async-start | bytes 2097152 | tf_op jit(solution)/shard_map/all_to_all | solution.py:127
  487.5 27.8 %all-to-all-done.4 = bf16[3,16,8192]{2,0,1:T(4,128)(2,1)} async-done(((bf16[3,16,8192]{2,0,1:T(4,128)(2,1)}), bf16[3,16,8192]{2,0,1:T(4,128)(2,1)}, u32[]{:S(2)}, u32[]{:S(2)}) %all-to-all-start.4) | async-done | bytes 786464 | tf_op jit(solution)/shard_map/all_to_all | solution.py:127
  515.4 1.8 copy.103
  518.9 1.7 reshape.145
  (96 shorter events, 31.7 us)
Async XLA Ops:
  6.5 210.2 %copy-start = (bf16[1,128,8192]{2,1,0:T(8,128)(2,1)S(1)}, bf16[1,128,8192]{2,1,0:T(8,128)(2,1)}, u32[]{:S(2)}) copy-start(bf16[1,128,8192]{2,1,0:T(8,128)(2,1)} %param.31) | copy-start | bytes 6291460
  6.5 4.3 copy-start.3
  13.0 9.0 %collective-permute-start.3 = (f32[8,64,128]{2,1,0:T(8,128)S(1)}, f32[8,64,128]{2,1,0:T(8,128)S(1)}, u32[]{:S(2)}, u32[]{:S(2)}) collective-permute-start(f32[8,64,128]{2,1,0:T(8,128)S(1)} %get-tuple-element.48), channel_id=1, source_target_pairs={{0,16},{16,32},{32,48},{48,64},{64,80},{80,96},{96,112},{112,128},... | collective-permute-start | bytes 786440 | tf_op jit(solution)/shard_map/ppermute | solution.py:17
  17.0 5.0 collective-permute-start
  21.9 9.7 %copy-start.6 = (f32[8]{0:T(128)}, f32[8]{0:T(128)S(1)}, u32[]{:S(2)}) copy-start(f32[8]{0:T(128)S(1)} %collective-permute-done) | copy-start | bytes 100
  22.1 9.6 %collective-permute-start.4 = (f32[8,64,128]{2,1,0:T(8,128)S(1)}, f32[8,64,128]{2,1,0:T(8,128)S(1)}, u32[]{:S(2)}, u32[]{:S(2)}) collective-permute-start(f32[8,64,128]{2,1,0:T(8,128)S(1)} %multiply_add_fusion.3), channel_id=1, source_target_pairs={{0,32},{16,48},{32,64},{48,80},{64,96},{80,112},{96,128},{112,144}... | collective-permute-start | bytes 786440 | tf_op jit(solution)/shard_map/ppermute | solution.py:17
  31.7 11.8 %collective-permute-start.5 = (f32[8,64,128]{2,1,0:T(8,128)S(1)}, f32[8,64,128]{2,1,0:T(8,128)S(1)}, u32[]{:S(2)}, u32[]{:S(2)}) collective-permute-start(f32[8,64,128]{2,1,0:T(8,128)S(1)} %multiply_add_fusion.2), channel_id=1, source_target_pairs={{0,64},{16,80},{32,96},{48,112},{64,128},{80,144},{96,160},{112,17... | collective-permute-start | bytes 786440 | tf_op jit(solution)/shard_map/ppermute | solution.py:17
  40.6 2.3 collective-permute-start.1
  43.0 10.9 %copy-start.7 = (f32[8]{0:T(128)}, f32[8]{0:T(128)S(1)}, u32[]{:S(2)}) copy-start(f32[8]{0:T(128)S(1)} %collective-permute-done.1) | copy-start | bytes 100
  44.4 20.7 %collective-permute-start.6 = (f32[8,64,128]{2,1,0:T(8,128)}, f32[8,64,128]{2,1,0:T(8,128)}, u32[]{:S(2)}, u32[]{:S(2)}) collective-permute-start(f32[8,64,128]{2,1,0:T(8,128)} %multiply_add_fusion.1), channel_id=1, source_target_pairs={{0,128},{16,144},{32,160},{48,176},{64,192},{80,208},{96,224},{112... | collective-permute-start | bytes 786440 | tf_op jit(solution)/shard_map/ppermute | solution.py:17
  54.6 13.2 %copy-start.5 = (pred[128,128]{1,0:T(8,128)(4,1)S(1)}, pred[128,128]{1,0:T(8,128)(4,1)}, u32[]{:S(2)}) copy-start(pred[128,128]{1,0:T(8,128)(4,1)} %iota_compare_fusion) | copy-start | bytes 49156
  57.5 2.2 collective-permute-start.2
  60.4 4.0 collective-permute-start.7
  70.4 26.9 %copy-start.2 = (bf16[16,8192]{1,0:T(8,128)(2,1)S(1)}, bf16[16,8192]{1,0:T(8,128)(2,1)}, u32[]{:S(2)}) copy-start(bf16[16,8192]{1,0:T(8,128)(2,1)} %param.25) | copy-start | bytes 786436
  70.6 26.9 %copy-start.4 = (f32[8192]{0:T(1024)S(1)}, f32[8192]{0:T(1024)}, u32[]{:S(2)}) copy-start(f32[8192]{0:T(1024)} %param.26) | copy-start | bytes 98308
  71.4 25.7 %all-to-all-start = ((bf16[16,16,512]{2,1,0:T(8,128)(2,1)}), bf16[16,16,512]{2,1,0:T(8,128)(2,1)S(1)}, u32[]{:S(2)}, u32[]{:S(2)}) async-start(bf16[16,16,512]{2,1,0:T(8,128)(2,1)} %bitcast.10), calls=%async_computation | async-start | bytes 524288 | tf_op jit(solution)/shard_map/all_to_all | solution.py:88
  133.7 69.7 %all-to-all-start.2 = ((bf16[16,16,8192]{2,1,0:T(8,128)(2,1)}), bf16[16,16,8192]{2,1,0:T(8,128)(2,1)}, u32[]{:S(2)}, u32[]{:S(2)}) async-start(bf16[16,16,8192]{2,1,0:T(8,128)(2,1)} %stack.6), calls=%async_computation.2 | async-start | bytes 8388608 | tf_op jit(solution)/shard_map/all_to_all | solution.py:115
  207.7 140.0 %all-to-all-start.3 = ((bf16[16,32,8192]{2,1,0:T(8,128)(2,1)}), bf16[16,32,8192]{2,1,0:T(8,128)(2,1)}, u32[]{:S(2)}, u32[]{:S(2)}) async-start(bf16[16,32,8192]{2,1,0:T(8,128)(2,1)} %stack.7), calls=%async_computation.4 | async-start | bytes 16777216 | tf_op jit(solution)/shard_map/all_to_all | solution.py:115
  212.4 168.9 %reduce-scatter.3.cloned.1.call-start = ((), (), s32[]{:S(2)}) async-start(), calls=%async_computation.7 | async-start | bytes 4456448 | tf_op jit(solution)/shard_map/reduce_scatter | solution.py:122
  224.0 251.6 %reduce-scatter.5.cloned.1.call-start = ((), (), s32[]{:S(2)}) async-start(), calls=%async_computation.8 | async-start | bytes 8912896 | tf_op jit(solution)/shard_map/reduce_scatter | solution.py:122
  347.7 6.6 %copy-start.1 = (bf16[1,8192,128]{2,1,0:T(8,128)(2,1)S(1)}, bf16[1,8192,128]{2,1,0:T(8,128)(2,1)}, u32[]{:S(2)}) copy-start(bf16[1,8192,128]{2,1,0:T(8,128)(2,1)} %param.30) | copy-start | bytes 6291460
  476.8 10.7 %copy-start.8 = (f32[16,2]{0,1:T(2,128)S(1)}, f32[16,2]{0,1:T(2,128)}, u32[]{:S(2)}) copy-start(f32[16,2]{0,1:T(2,128)} %param.28) | copy-start | bytes 388
  478.5 36.9 %all-to-all-start.4 = ((bf16[3,16,8192]{2,0,1:T(4,128)(2,1)}), bf16[3,16,8192]{2,0,1:T(4,128)(2,1)}, u32[]{:S(2)}, u32[]{:S(2)}) async-start(bf16[3,16,8192]{2,0,1:T(4,128)(2,1)} %copy.102), calls=%async_computation.6 | async-start | bytes 2097152 | tf_op jit(solution)/shard_map/all_to_all | solution.py:127
Sparse Core Ops, SparseCore 0:
  224.2 157.1 reduce-scatter.2
  385.5 90.1 reduce-scatter.4
